TPU v7x, 128 devices: a whole 4x4x4 slice. The times are simulated.
128 devices in a mesh: group: 2 (over y_lo), row: 8 (over x, y_hi), head: 8 (over z, core).
Axes of the slice: x: 4, y: 4 (y_hi: 2, y_lo: 2; y = y_hi * 2 + y_lo), z: 4, core: 2. Of those that a mesh axis runs over, the one named last changes fastest.
Arguments:
- latent: bfloat16 [2048, 3072], P('row', 'head'), may hold values from -6 to 6
- hint: bfloat16 [2048, 3072], P('row', 'head'), may hold values from -6 to 6
- timestep: int32 [1], replicated, may hold values from 0 to 7
- modulation: float32 [2, 8, 3, 3072], P('group'), may hold values from -3 to 3
- qkv_weight: bfloat16 [2, 3, 3072, 3072], P('group', None, None, 'head'), may hold values from -0.109375 to 0.109375
- out_weight: bfloat16 [2, 3072, 3072], P('group', None, 'head'), may hold values from -0.109375 to 0.109375
- zero_weight: bfloat16 [3072, 3072], P(None, 'head'), may hold values from -0.109375 to 0.109375
- cotangent: bfloat16 [2048, 3072], P('row', 'head'), may hold values from -6 to 6
Outputs:
- mixed: bfloat16 [2048, 3072], P('row', 'head')
- latent_grad: float32 [8, 2, 128, 3072], P('row', 'group', None, 'head')
- hint_grad: float32 [8, 2, 128, 3072], P('row', 'group', None, 'head')
- qkv_grad: float32 [3072, 3, 3072], P(('group', 'row'), None, 'head')
- out_grad: float32 [3072, 3072], P(('group', 'row'), 'head')
- zero_grad: float32 [3072, 3072], P(('group', 'row'), 'head')
All inputs are finite; a program needn't handle non-finite values.
Results may differ from a plain program's by a relative error of at most 0.015.
Values may be sent and summed in bfloat16 or wider, within the bound.
No kernel may reach another device: no remote copies, remote signals or barrier semaphores. Data moves between devices by JAX's collectives and lax.ppermute only.
A program may use at most 128 MiB of HBM per device.

v0:
```python
import functools

import jax
import jax.numpy as jnp
from jax import lax
from jax.experimental import pallas as pl
from jax.experimental.pallas import tpu as pltpu
from jax.sharding import Mesh
from jax.sharding import PartitionSpec as P


HD = 128
ROW = ("row_0", "row_1")
HEAD = ("z", "core")
GROUP_ROW = ("group", "row_0", "row_1")
YAX = ("group", "row_1")
EPS = 1e-06
F32 = jnp.float32
BF16 = jnp.bfloat16
ANY = pl.BlockSpec(memory_space=pl.ANY)


def dot_nn(a, b):
    return lax.dot_general(a, b, (((1,), (0,)), ((), ())), preferred_element_type=F32)


def dot_nt(a, b):
    return lax.dot_general(a, b, (((1,), (1,)), ((), ())), preferred_element_type=F32)


def moved(array, axis, pairs):
    return lax.ppermute(array, axis, pairs)


def swap(array, axis, size, distance):
    return moved(array, axis, [(i, i ^ distance) for i in range(size)])


def cost(flops, size, trans=0):
    return pl.CostEstimate(flops=flops, bytes_accessed=size, transcendentals=trans)


def shaped(shape, dtype=BF16):
    return jax.ShapeDtypeStruct(shape, dtype)


def full(shape):
    return pl.BlockSpec(shape, lambda *a: (0,) * len(shape))


def run(body, place, args, specs, outs, scratch, estimate):
    return pl.pallas_call(
        body,
        grid_spec=pltpu.PrefetchScalarGridSpec(
            num_scalar_prefetch=1,
            grid=(1,),
            in_specs=specs,
            out_specs=[full(o.shape) for o in outs],
            scratch_shapes=scratch,
        ),
        out_shape=outs,
        cost_estimate=estimate,
    )(place, *args)


def gather_head(own):
    mine = [own] + [swap(own, "z", 4, d) for d in (1, 2, 3)]
    pieces = []
    for a in mine:
        pieces += [a, swap(a, "core", 2, 1)]
    return pieces


def sum_head(own, other):
    got = swap(other, "core", 2, 1)
    sums = [own[d].astype(F32) + got[d].astype(F32) for d in range(4)]
    total = sums[0]
    for d in (1, 2, 3):
        total = total + swap(sums[d].astype(BF16), "z", 4, d).astype(F32)
    return total


def lanes(index, width):
    return pl.ds(pl.multiple_of(index * width, 128), width)


def lay_out(place, pieces, whole):
    width = pieces[0].shape[1]
    for p, piece in enumerate(pieces):
        whole[:, lanes(place[0] ^ p, width)] = piece[...]


def norm_qkv_kernel(place, *refs):
    pieces, (mods, w) = refs[:8], refs[8:10]
    cols, qkv, stats = refs[10:13]
    whole, wbuf, sems = refs[13:]
    tok, width = pieces[0].shape

    def fetch(c):
        return pltpu.make_async_copy(w.at[c], wbuf.at[c], sems.at[c])

    for c in range(3):
        fetch(c).start()
    lay_out(place, pieces, whole)
    features = 8 * width
    zero = jnp.zeros((tok, 1), F32)

    def chunk(k):
        return whole[:, lanes(k, width)].astype(F32)

    mean = lax.fori_loop(
        0, 8, lambda k, t: t + jnp.sum(chunk(k), axis=-1, keepdims=True), zero, unroll=2
    ) / features

    def squares(k, t):
        c = chunk(k) - mean
        return t + jnp.sum(c * c, axis=-1, keepdims=True)

    rstd = lax.rsqrt(lax.fori_loop(0, 8, squares, zero, unroll=2) / features + EPS)
    stats[0] = jnp.broadcast_to(mean, stats.shape[1:])
    stats[1] = jnp.broadcast_to(rstd, stats.shape[1:])

    @pl.loop(0, 8, unroll=2)
    def _(k):
        at = lanes(k, width)
        nhat = (chunk(k) - mean) * rstd
        n = (nhat * (1.0 + mods[1:2, at]) + mods[0:1, at]).astype(BF16)
        whole[:, at] = n

        @pl.when(place[1] == k // 4)
        def _():
            cols[place[2] ^ (k % 4)] = n

    @pl.loop(0, 3)
    def _(c):
        fetch(c).wait()
        qkv[c] = dot_nn(whole[...], wbuf[c]).astype(BF16)


def norm_qkv(place, pieces, mods, w):
    tok, width = pieces[0].shape
    return run(
        norm_qkv_kernel,
        place,
        (*pieces, mods, w),
        [full((tok, width))] * 8 + [full(mods.shape), ANY],
        [shaped((4, tok, width)), shaped((3, tok, width)), shaped((2, tok, 128), F32)],
        [
            pltpu.VMEM((tok, 8 * width), BF16),
            pltpu.VMEM(w.shape, BF16),
            pltpu.SemaphoreType.DMA((3,)),
        ],
        cost(2 * tok * 8 * width * 3 * width, 12 * 2**20),
    )


def hint_kernel(place, *refs):
    pieces, (mods, w) = refs[:8], refs[8:10]
    incoming, gated, cols = refs[10:13]
    whole, wbuf, sem = refs[13:]
    width = pieces[0].shape[1]
    copy = pltpu.make_async_copy(w, wbuf, sem.at[0])
    copy.start()
    lay_out(place, pieces, whole)
    for d in range(4):
        cols[d] = whole[:, lanes(place[1] * 4 + (place[2] ^ d), width)]
    copy.wait()
    back = dot_nn(whole[...], wbuf[...]).astype(BF16)
    got = jnp.where(place[3] == 0, back, pieces[0][...])
    incoming[...] = got
    gate = mods[2:3, lanes(place[0], width)]
    gated[...] = (gate * got.astype(F32)).astype(BF16)


def hint_back(place, pieces, mods, w):
    tok, width = pieces[0].shape
    return run(
        hint_kernel,
        place,
        (*pieces, mods, w),
        [full((tok, width))] * 8 + [full(mods.shape), ANY],
        [shaped((tok, width)), shaped((tok, width)), shaped((4, tok, width))],
        [
            pltpu.VMEM((tok, 8 * width), BF16),
            pltpu.VMEM(w.shape, BF16),
            pltpu.SemaphoreType.DMA((1,)),
        ],
        cost(2 * tok * 8 * width * width, 6 * 2**20),
    )


def branch_grad_kernel(place, *refs):
    pieces, (w, ncols, ccols) = refs[:8], refs[8:11]
    out, packs = refs[11], refs[12:16]
    whole, wbuf, sem = refs[16:]
    width = pieces[0].shape[1]
    copy = pltpu.make_async_copy(w, wbuf, sem.at[0])
    copy.start()
    lay_out(place, pieces, whole)
    for d in range(4):
        packs[d][0] = ncols[d]

        @pl.when(place[3] == 0)
        def _():
            packs[d][1] = whole[:, lanes(place[1] * 4 + (place[2] ^ d), width)]

        @pl.when(place[3] != 0)
        def _():
            packs[d][1] = ccols[d]

    copy.wait()
    out[...] = dot_nn(whole[...], wbuf[...]).astype(BF16)


def branch_grad(place, pieces, w, ncols, ccols):
    tok, width = pieces[0].shape
    return run(
        branch_grad_kernel,
        place,
        (*pieces, w, ncols, ccols),
        [full((tok, width))] * 8 + [ANY, full(ncols.shape), full(ccols.shape)],
        [shaped((tok, width))] + [shaped((2, tok, width))] * 4,
        [
            pltpu.VMEM((tok, 8 * width), BF16),
            pltpu.VMEM(w.shape, BF16),
            pltpu.SemaphoreType.DMA((1,)),
        ],
        cost(2 * tok * 8 * width * width, 8 * 2**20),
    )


def spread_kernel(place, a, w, own, other, wbuf, sems):
    width = a.shape[1]
    pair = 2 * width
    copies = []
    for d in range(4):
        rows = pl.ds(pl.multiple_of(((place[0] // 2) ^ d) * pair, pair), pair)
        copies.append(pltpu.make_async_copy(w.at[rows], wbuf.at[d], sems.at[d]))
        copies[-1].start()
    for d in range(4):
        copies[d].wait()
        part = dot_nt(a[...], wbuf[d]).astype(BF16)

        @pl.when(place[1] == 0)
        def _():
            own[d] = part[:, :width]
            other[d] = part[:, width:]

        @pl.when(place[1] != 0)
        def _():
            own[d] = part[:, width:]
            other[d] = part[:, :width]


def spread(place, a, w):
    tok, width = a.shape
    return run(
        spread_kernel,
        place,
        (a, w),
        [full((tok, width)), ANY],
        [shaped((4, tok, width))] * 2,
        [pltpu.VMEM((4, 2 * width, width), BF16), pltpu.SemaphoreType.DMA((4,))],
        cost(2 * tok * 8 * width * width, 6 * 2**20),
    )


def spread_norm_kernel(place, grads, w, mods, stats, *refs):
    pieces, (own, other, sums, whole, wbuf, sems) = refs[:8], refs[8:]
    tok, width = pieces[0].shape
    pair = 2 * width

    def fetch(d):
        rows = pl.ds(pl.multiple_of(((place[0] // 2) ^ d) * pair, pair), pair)
        return pltpu.make_async_copy(w.at[:, rows], wbuf.at[d], sems.at[d])

    for d in range(4):
        fetch(d).start()
    lay_out(place, pieces, whole)
    mean, rstd = stats[0, :, :1], stats[1, :, :1]
    zero = jnp.zeros((tok, 1), F32)

    def step(d, totals):
        first, second = totals
        fetch(d).wait()
        part = (
            dot_nt(grads[0], wbuf[d, 0])
            + dot_nt(grads[1], wbuf[d, 1])
            + dot_nt(grads[2], wbuf[d, 2])
        )
        low, high = part[:, :width].astype(BF16), part[:, width:].astype(BF16)

        @pl.when(place[1] == 0)
        def _():
            own[d] = low
            other[d] = high

        @pl.when(place[1] != 0)
        def _():
            own[d] = high
            other[d] = low

        at = lanes((place[0] // 2) ^ d, pair)
        scaled = part * (1.0 + mods[1:2, at])
        nhat = (whole[:, at].astype(F32) - mean) * rstd
        first += jnp.sum(scaled, axis=-1, keepdims=True)
        second += jnp.sum(scaled * nhat, axis=-1, keepdims=True)
        return first, second

    first, second = lax.fori_loop(0, 4, step, (zero, zero))
    lane = lax.broadcasted_iota(jnp.int32, (tok, 128), 1)
    both = jnp.where(lane == 0, first, jnp.where(lane == 1, second, 0.0))
    sums[...] = jnp.transpose(both)[:8]


def spread_norm(place, grads, w, mods, stats, pieces):
    _, tok, width = grads.shape
    return run(
        spread_norm_kernel,
        place,
        (grads, w, mods, stats, *pieces),
        [full(grads.shape), ANY, full(mods.shape), full(stats.shape)]
        + [full((tok, width))] * 8,
        [shaped((4, tok, width))] * 2 + [shaped((8, tok), F32)],
        [
            pltpu.VMEM((tok, 8 * width), BF16),
            pltpu.VMEM((4, 3, 2 * width, width), BF16),
            pltpu.SemaphoreType.DMA((4,)),
        ],
        cost(6 * tok * 8 * width * width, 14 * 2**20),
    )


def attention_kernel(scaling, q_ref, g_ref, k_ref, v_ref, o_ref, dq_ref, dkv_ref, scores):
    q, g = q_ref[0], g_ref[...]
    blocks, _, tok, _ = k_ref.shape
    peak = None
    for b in range(blocks):
        s = dot_nt(k_ref[b, 0], q) * scaling
        scores[b] = s
        top = jnp.max(s, axis=0, keepdims=True)
        peak = top if peak is None else jnp.maximum(peak, top)
    total = jnp.zeros((1, tok), F32)
    acc = jnp.zeros((HD, tok), F32)
    for b in range(blocks):
        w = jnp.exp(scores[b] - peak)
        scores[b] = w
        total += jnp.sum(w, axis=0, keepdims=True)
        acc += dot_nn(jnp.transpose(v_ref[b, 0]), w.astype(BF16))
    out_t = (acc / total).astype(BF16).astype(F32)
    o_ref[...] = jnp.transpose(out_t).astype(BF16)
    dsum = jnp.sum(jnp.transpose(g.astype(F32)) * out_t, axis=0, keepdims=True)
    inverse = 1.0 / total
    dq = jnp.zeros((HD, tok), F32)
    for b in range(blocks):
        probs = scores[b] * inverse
        dprobs = dot_nt(v_ref[b, 0], g)
        ds = (probs * (dprobs - dsum)).astype(BF16)
        dkv_ref[b, 0] = (dot_nn(ds, q) * scaling).astype(BF16)
        dkv_ref[b, 1] = dot_nn(probs.astype(BF16), g).astype(BF16)
        dq += dot_nn(jnp.transpose(k_ref[b, 0]), ds)
    dq_ref[...] = (jnp.transpose(dq) * scaling).astype(BF16)


def attention(qkv, grad, kv):
    tok, width = grad.shape
    heads, blocks = width // HD, kv.shape[0]
    one = pl.BlockSpec((tok, HD), lambda j: (0, j))
    return pl.pallas_call(
        functools.partial(attention_kernel, HD**-0.5),
        grid=(heads,),
        in_specs=[
            pl.BlockSpec((1, tok, HD), lambda j: (0, 0, j)),
            one,
            pl.BlockSpec((blocks, 1, tok, HD), lambda j: (0, 0, 0, j)),
            pl.BlockSpec((blocks, 1, tok, HD), lambda j: (0, 1, 0, j)),
        ],
        out_specs=[one, one, pl.BlockSpec((blocks, 2, tok, HD), lambda j: (0, 0, 0, j))],
        out_shape=[
            shaped((tok, width)),
            shaped((tok, width)),
            shaped((blocks, 2, tok, width)),
        ],
        scratch_shapes=[pltpu.VMEM((blocks, tok, tok), F32)],
        cost_estimate=cost(12 * tok * blocks * tok * width, 8 * 2**20, tok * blocks * tok * heads),
    )(qkv, grad, kv, kv)


def token_sum_kernel(place, *refs):
    own, other, xs, out, turned = refs[:4], refs[4:8], refs[8:12], refs[12], refs[13]
    i, c = pl.program_id(0), pl.program_id(1)
    tok = own[0].shape[1]

    for half, cols in enumerate((own, other)):

        @pl.when((c == 0) & (i == half))
        def _():
            for d in range(4):
                turned[:, d * tok : (d + 1) * tok] = jnp.transpose(cols[d][0])

    acc = dot_nn(turned[:, :tok], xs[0][0])
    for d in range(1, 4):
        acc += dot_nn(turned[:, d * tok : (d + 1) * tok], xs[d][0])
    acc = acc.astype(BF16)
    half = acc.shape[0] // 2

    @pl.when(place[5] == 0)
    def _():
        out[0, 0, 0] = acc[:half]
        out[0, 1, 0] = acc[half:]

    @pl.when(place[5] != 0)
    def _():
        out[0, 0, 0] = acc[half:]
        out[0, 1, 0] = acc[:half]


def token_sum(place, which, own, other, xs):
    _, tok, cols = own[0].shape
    kinds, _, width = xs[0].shape
    column = pl.BlockSpec((1, tok, cols), lambda i, c, s: (which, 0, 0))
    return pl.pallas_call(
        token_sum_kernel,
        grid_spec=pltpu.PrefetchScalarGridSpec(
            num_scalar_prefetch=1,
            grid=(2, kinds),
            in_specs=[column] * 8
            + [pl.BlockSpec((1, tok, width), lambda i, c, s: (c, 0, 0))] * 4,
            out_specs=pl.BlockSpec(
                (1, 2, 1, cols // 2, width), lambda i, c, s: (i ^ s[4], 0, c, 0, 0)
            ),
            scratch_shapes=[pltpu.VMEM((cols, 4 * tok), BF16)],
        ),
        out_shape=shaped((2, 2, kinds, cols // 2, width)),
        cost_estimate=cost(16 * tok * cols * kinds * width, 6 * 2**20),
    )(place, *own, *other, *xs)


def along_x(array):
    return [array] + [swap(array, "row_0", 4, d) for d in (1, 2, 3)]


def on_device(latent, hint, timestep, modulation, qkv_weight, out_weight, zero_weight, cotangent):
    tok, width = latent.shape
    x_pos, y_pos = lax.axis_index("row_0"), lax.axis_index("row_1")
    core_pos, group_pos = lax.axis_index("core"), lax.axis_index("group")
    head_pos = lax.axis_index("z") * 2 + core_pos
    control = group_pos == 0
    place = jnp.stack(
        [head_pos, core_pos, x_pos, group_pos, core_pos ^ group_pos, y_pos]
    ).astype(jnp.int32)
    w_qkv, w_out = qkv_weight[0], out_weight[0]
    full_width = w_out.shape[0]

    chosen = lax.dynamic_index_in_dim(modulation[0], timestep[0], 0, keepdims=False)
    mods_dev = lax.dynamic_slice_in_dim(chosen, head_pos * width, width, 1)
    scale_dev, gate_dev = mods_dev[1], mods_dev[2]

    summed = (latent.astype(F32) + hint.astype(F32)).astype(BF16)
    inputs = jnp.where(control, summed, latent)
    whole = gather_head(inputs)
    cot_late = lax.optimization_barrier((cotangent, whole[2], whole[4], whole[6]))[0]
    cot_full = gather_head(cot_late)
    ncols, qkv, stats = norm_qkv(place, whole, chosen, w_qkv)
    kv_full = lax.all_to_all(
        jnp.broadcast_to(qkv[1:], (8, 2, tok, width)), ROW, split_axis=0, concat_axis=0, tiled=True
    )

    incoming, gated, ccols = hint_back(place, cot_full, chosen, zero_weight)
    gated_full = gather_head(gated)
    attn_grad, *packs = branch_grad(place, gated_full, w_out, ncols, ccols)
    cols = packs[:1] + [swap(packs[d], "row_0", 4, d) for d in (1, 2, 3)]
    cols_other = [swap(a, "core", 2, 1) for a in cols]

    attn, dquery, dkv = attention(qkv, attn_grad, kv_full)
    dkv_all = lax.all_to_all(dkv, ROW, split_axis=0, concat_axis=0, tiled=True)

    branch = sum_head(*spread(place, attn, w_out))
    state = (inputs.astype(F32) + gate_dev * branch).astype(BF16)
    other_state = swap(state, "group", 2, 1)
    control_out = jnp.where(control, state, other_state)
    main_out = jnp.where(control, other_state, state)
    zero_own, zero_other = spread(place, control_out, zero_weight)

    dkv_all, zero_own = lax.optimization_barrier((dkv_all, zero_own))
    dkv_sum = jnp.sum(dkv_all.astype(F32), axis=0).astype(BF16)
    grads = jnp.concatenate([dquery[None], dkv_sum])
    grads_x = along_x(grads)
    projected = sum_head(zero_own, zero_other)
    mixed = (main_out.astype(F32) + projected).astype(BF16)
    own_terms, other_terms, sums = spread_norm(place, grads, w_qkv, chosen, stats, whole)
    for axis, size, d in (("core", 2, 1), ("z", 4, 1), ("z", 4, 2)):
        sums = sums + swap(sums, axis, size, d)
    dnorm = sum_head(own_terms, other_terms)
    mean, rstd = stats[0, :, :1], stats[1, :, :1]
    nhat_dev = (inputs.astype(F32) - mean) * rstd
    first = sums[0][:, None] / full_width
    second = sums[1][:, None] / full_width
    d_in = incoming.astype(F32) + rstd * (dnorm * (1.0 + scale_dev) - first - nhat_dev * second)
    half = tok // 2
    own_half = lax.dynamic_slice_in_dim(d_in, group_pos * half, half, 0)
    sent_half = lax.dynamic_slice_in_dim(d_in, (1 - group_pos) * half, half, 0)
    other_half = swap(sent_half, "group", 2, 1)
    latent_grad = (own_half + other_half)[None, None]
    hint_grad = jnp.where(control, own_half, other_half)[None, None]

    attn_or_state = jnp.where(control, attn, control_out)
    side = token_sum(place, 1, cols, cols_other, along_x(attn_or_state[None]))
    near = side[0, 0, 0].astype(F32) + swap(side[0, 1, 0], "row_1", 2, 1).astype(F32)
    far = swap(side[1, 0, 0], "group", 2, 1).astype(F32) + moved(
        side[1, 1, 0], YAX, [(0, 3), (1, 2), (2, 1), (3, 0)]
    ).astype(F32)
    out_grad = jnp.where(control, near, far)
    zero_grad = jnp.where(control, far, near)

    main = token_sum(place, 0, cols, cols_other, grads_x)
    near = main[0, 0].astype(F32) + moved(main[0, 1], YAX, [(0, 1), (1, 0)]).astype(F32)
    far = moved(main[1, 0], YAX, [(0, 2), (1, 3)]).astype(F32) + moved(
        main[1, 1], YAX, [(0, 3), (1, 2)]
    ).astype(F32)
    qkv_grad = jnp.where(control, near, far).transpose(1, 0, 2)
    return (mixed, latent_grad, hint_grad, qkv_grad, out_grad, zero_grad)


def solution(mesh):
    torus = Mesh(
        mesh.devices.reshape(mesh.shape["group"], 4, 2, 4, 2),
        ("group", "row_0", "row_1", "z", "core"),
    )

    return jax.shard_map(
        on_device,
        mesh=torus,
        in_specs=(
            P(ROW, HEAD),
            P(ROW, HEAD),
            P(),
            P("group", None, None, None),
            P("group", None, None, HEAD),
            P("group", None, HEAD),
            P(None, HEAD),
            P(ROW, HEAD),
        ),
        out_specs=(
            P(ROW, HEAD),
            P(ROW, "group", None, HEAD),
            P(ROW, "group", None, HEAD),
            P(GROUP_ROW, None, HEAD),
            P(GROUP_ROW, HEAD),
            P(GROUP_ROW, HEAD),
        ),
        check_vma=False,
    )
```

profile of v0, /device:TPU:1, one launch (start us, length us, event | category | flops | bytes accessed | tf_op | source)
XLA Modules:
  0.0 280.9 jit_solution(3723885202349899310)
XLA Ops:
  4.4 3.3 %collective-permute-start.3 = (bf16[256,384]{1,0:T(8,128)(2,1)S(1)}, bf16[256,384]{1,0:T(8,128)(2,1)S(1)}, u32[]{:S(2)}, u32[]{:S(2)}) collective-permute-start(bf16[256,384]{1,0:T(8,128)(2,1)S(1)} %fusion.19.refs_0_), channel_id=1, source_target_pairs={{0,4},{2,6},{4,0},{6,2},{1,5},{3,7},{5,1},{7,3},{8,12},{10,14},{12... | collective-permute-start | bytes 589832 | tf_op jit(solution)/shard_map/ppermute | solution.py:32
  11.1 5.2 %collective-permute-done.3.refs_4_ = bf16[256,384]{1,0:T(8,128)(2,1)S(1)} collective-permute-done((bf16[256,384]{1,0:T(8,128)(2,1)S(1)}, bf16[256,384]{1,0:T(8,128)(2,1)S(1)}, u32[]{:S(2)}, u32[]{:S(2)}) %collective-permute-start.3) | collective-permute-done | bytes 196640 | tf_op jit(solution)/shard_map/ppermute | solution.py:32
  23.6 8.4 %shard_map.127 = (bf16[4,256,384]{2,1,0:T(8,128)(2,1)}, bf16[3,256,384]{2,1,0:T(8,128)(2,1)}, f32[2,256,128]{2,1,0:T(8,128)}) custom-call(s32[6]{0:T(128)} %stack.27.place, bf16[256,384]{1,0:T(8,128)(2,1)} %copy-done.1, bf16[256,384]{1,0:T(8,128)(2,1)} %copy-done.15, bf16[256,384]{1,0:T(8,128)(2,1)} %copy-done.12, bf16[256,384]{1,0:T(8,128)(2,1)} %copy-done.16, ...), custom_call_target="tpu_custom_call" | custom-call | flops 1811939328 | bytes 12582912 | tf_op jit(solution)/shard_map/pallas_call | solution.py:52
  35.2 6.8 %all-to-all-start = ((bf16[8,2,256,384]{3,2,1,0:T(8,128)(2,1)}), bf16[8,2,256,384]{3,2,1,0:T(8,128)(2,1)S(1)}, u32[]{:S(2)}, u32[]{:S(2)}) async-start(bf16[8,2,256,384]{3,2,1,0:T(8,128)(2,1)} %broadcast_in_dim.16), calls=%async_computation | async-start | bytes 6291456 | tf_op jit(solution)/shard_map/all_to_all | solution.py:465
  57.5 5.8 %shard_map.128 = (bf16[256,384]{1,0:T(8,128)(2,1)}, bf16[256,384]{1,0:T(8,128)(2,1)}, bf16[4,256,384]{2,1,0:T(8,128)(2,1)}) custom-call(s32[6]{0:T(128)} %stack.27.place, bf16[256,384]{1,0:T(8,128)(2,1)} %refs_0_, bf16[256,384]{1,0:T(8,128)(2,1)} %copy-done.29, bf16[256,384]{1,0:T(8,128)(2,1)} %copy-done.24, bf16[256,384]{1,0:T(8,128)(2,1)} %copy-done.31, ...), custom_call_target="tpu_custom_call" | custom-call | flops 603979776 | bytes 6291456 | tf_op jit(solution)/shard_map/pallas_call | solution.py:52
  63.4 3.8 %collective-permute-start.17 = (bf16[256,384]{1,0:T(8,128)(2,1)}, bf16[256,384]{1,0:T(8,128)(2,1)S(1)}, u32[]{:S(2)}, u32[]{:S(2)}) collective-permute-start(bf16[256,384]{1,0:T(8,128)(2,1)} %get-tuple-element.32.refs_0_), channel_id=1, source_target_pairs={{0,4},{2,6},{4,0},{6,2},{1,5},{3,7},{5,1},{7,3},{8,12},{10,14},{12... | collective-permute-start | bytes 589832 | tf_op jit(solution)/shard_map/ppermute | solution.py:32
  71.5 5.1 %collective-permute-done.17.refs_4_ = bf16[256,384]{1,0:T(8,128)(2,1)S(1)} collective-permute-done((bf16[256,384]{1,0:T(8,128)(2,1)}, bf16[256,384]{1,0:T(8,128)(2,1)S(1)}, u32[]{:S(2)}, u32[]{:S(2)}) %collective-permute-start.17) | collective-permute-done | bytes 196640 | tf_op jit(solution)/shard_map/ppermute | solution.py:32
  82.0 6.0 %shard_map.129 = (bf16[256,384]{1,0:T(8,128)(2,1)}, bf16[2,256,384]{2,1,0:T(8,128)(2,1)}, bf16[2,256,384]{2,1,0:T(8,128)(2,1)}, bf16[2,256,384]{2,1,0:T(8,128)(2,1)}, bf16[2,256,384]{2,1,0:T(8,128)(2,1)}) custom-call(s32[6]{0:T(128)} %stack.27.place, bf16[256,384]{1,0:T(8,128)(2,1)} %get-tuple-element.32.refs_0_, bf16[256,384]{1,0:T(8,128)(2,1)} %copy-done.27, ...), custom_call_target="tpu_custom_call" | custom-call | flops 603979776 | bytes 8388608 | tf_op jit(solution)/shard_map/pallas_call | solution.py:52
  89.7 10.5 %shard_map.130 = (bf16[256,384]{1,0:T(8,128)(2,1)}, bf16[256,384]{1,0:T(8,128)(2,1)}, bf16[8,2,256,384]{3,2,1,0:T(8,128)(2,1)}) custom-call(bf16[3,256,384]{2,1,0:T(8,128)(2,1)} %get-tuple-element.30.q_ref, bf16[256,384]{1,0:T(8,128)(2,1)} %get-tuple-element.35.g_ref, bf16[8,2,256,384]{3,2,1,0:T(8,128)(2,1)} %copy-done.4, bf16[8,2,256,384]{3,2,1,0:T(8,128)(2,1)} %copy-done.4), custom_call_target="tpu_custom_call" | custom-call | flops 2415919104 | bytes 8388608 | tf_op jit(solution)/shard_map/pallas_call | solution.py:369
  100.2 6.6 %all-to-all-start.1 = ((bf16[8,2,256,384]{3,2,1,0:T(8,128)(2,1)}), bf16[8,2,256,384]{3,2,1,0:T(8,128)(2,1)S(1)}, u32[]{:S(2)}, u32[]{:S(2)}) async-start(bf16[8,2,256,384]{3,2,1,0:T(8,128)(2,1)} %get-tuple-element.39), calls=%async_computation.1 | async-start | bytes 6291456 | tf_op jit(solution)/shard_map/all_to_all | solution.py:476
  106.8 6.0 %shard_map.131 = (bf16[4,256,384]{2,1,0:T(8,128)(2,1)}, bf16[4,256,384]{2,1,0:T(8,128)(2,1)}) custom-call(s32[6]{0:T(128)} %stack.27.place, bf16[256,384]{1,0:T(8,128)(2,1)} %get-tuple-element.36.a, bf16[3072,384]{1,0:T(8,128)(2,1)} %bitcast.103), custom_call_target="tpu_custom_call" | custom-call | flops 603979776 | bytes 6291456 | tf_op jit(solution)/shard_map/pallas_call | solution.py:52
  118.6 3.2 %collective-permute-start.22 = (bf16[256,384]{1,0:T(8,128)(2,1)S(1)}, bf16[256,384]{1,0:T(8,128)(2,1)}, u32[]{:S(2)}, u32[]{:S(2)}) collective-permute-start(bf16[256,384]{1,0:T(8,128)(2,1)S(1)} %get-tuple-element.69), channel_id=1, source_target_pairs={{0,2},{2,0},{4,6},{6,4},{1,3},{3,1},{5,7},{7,5},{8,10},{10,8},{12,... | collective-permute-start | bytes 589832 | tf_op jit(solution)/shard_map/ppermute | solution.py:32
  126.9 3.9 %collective-permute-done.24 = bf16[256,384]{1,0:T(8,128)(2,1)} collective-permute-done((bf16[256,384]{1,0:T(8,128)(2,1)}, bf16[256,384]{1,0:T(8,128)(2,1)}, u32[]{:S(2)}, u32[]{:S(2)}) %collective-permute-start.24) | collective-permute-done | bytes 196640 | tf_op jit(solution)/shard_map/ppermute | solution.py:32
  137.1 21.6 %collective-permute-done.38.refs_1_ = bf16[2,256,384]{2,1,0:T(8,128)(2,1)} collective-permute-done((bf16[2,256,384]{2,1,0:T(8,128)(2,1)}, bf16[2,256,384]{2,1,0:T(8,128)(2,1)}, u32[]{:S(2)}, u32[]{:S(2)}) %collective-permute-start.38) | collective-permute-done | bytes 393248 | tf_op jit(solution)/shard_map/ppermute | solution.py:32
  161.2 7.6 %collective-permute-done.39.refs_2_ = bf16[2,256,384]{2,1,0:T(8,128)(2,1)} collective-permute-done((bf16[2,256,384]{2,1,0:T(8,128)(2,1)}, bf16[2,256,384]{2,1,0:T(8,128)(2,1)}, u32[]{:S(2)}, u32[]{:S(2)}) %collective-permute-start.39) | collective-permute-done | bytes 393248 | tf_op jit(solution)/shard_map/ppermute | solution.py:32
  175.9 5.9 %shard_map.132 = (bf16[4,256,384]{2,1,0:T(8,128)(2,1)}, bf16[4,256,384]{2,1,0:T(8,128)(2,1)}) custom-call(s32[6]{0:T(128)} %stack.27.place, bf16[256,384]{1,0:T(8,128)(2,1)} %get-tuple-element.59.a, bf16[3072,384]{1,0:T(8,128)(2,1)} %w.1), custom_call_target="tpu_custom_call" | custom-call | flops 603979776 | bytes 6291456 | tf_op jit(solution)/shard_map/pallas_call | solution.py:52
  185.4 4.9 %shard_map.135 = bf16[2,2,1,192,384]{4,3,2,1,0:T(8,128)(2,1)} custom-call(s32[6]{0:T(128)} %stack.27.place, bf16[2,256,384]{2,1,0:T(8,128)(2,1)} %get-tuple-element.50.refs_0_, bf16[2,256,384]{2,1,0:T(8,128)(2,1)} %collective-permute-done.38.refs_1_, bf16[2,256,384]{2,1,0:T(8,128)(2,1)} %collective-permute-done.39.refs_2_, ...), custom_call_target="tpu_custom_call" | custom-call | flops 603979776 | bytes 6291456 | tf_op jit(solution)/shard_map/pallas_call | solution.py:422
  199.3 9.5 %shard_map.133 = (bf16[4,256,384]{2,1,0:T(8,128)(2,1)}, bf16[4,256,384]{2,1,0:T(8,128)(2,1)}, f32[8,256]{1,0:T(8,128)}) custom-call(s32[6]{0:T(128)} %stack.27.place, bf16[3,256,384]{2,1,0:T(8,128)(2,1)} %pad_maximum_fusion.grads.refs_8_, bf16[3,3072,384]{2,1,0:T(8,128)(2,1)} %bitcast.101, f32[3,3072]{1,0:T(4,128)} %bitcast.106, ...), custom_call_target="tpu_custom_call" | custom-call | flops 1811939328 | bytes 14680064 | tf_op jit(solution)/shard_map/pallas_call | solution.py:52
  213.2 3.1 %collective-permute-start.46 = (bf16[3,256,384]{2,1,0:T(8,128)(2,1)S(1)}, bf16[3,256,384]{2,1,0:T(8,128)(2,1)S(1)}, u32[]{:S(2)}, u32[]{:S(2)}) collective-permute-start(bf16[3,256,384]{2,1,0:T(8,128)(2,1)S(1)} %copy-done), channel_id=1, source_target_pairs={{0,32},{16,48},{32,0},{48,16},{1,33},{17,49},{33,1},{49,17},{2,34}... | collective-permute-start | bytes 1769480 | tf_op jit(solution)/shard_map/ppermute | solution.py:32
  228.8 13.3 %collective-permute-done.46.refs_10_ = bf16[3,256,384]{2,1,0:T(8,128)(2,1)S(1)} collective-permute-done((bf16[3,256,384]{2,1,0:T(8,128)(2,1)S(1)}, bf16[3,256,384]{2,1,0:T(8,128)(2,1)S(1)}, u32[]{:S(2)}, u32[]{:S(2)}) %collective-permute-start.46) | collective-permute-done | bytes 589856 | tf_op jit(solution)/shard_map/ppermute | solution.py:32
  244.2 8.8 %shard_map.134 = bf16[2,2,3,192,384]{4,3,2,1,0:T(8,128)(2,1)} custom-call(s32[6]{0:T(128)} %stack.27.place, bf16[2,256,384]{2,1,0:T(8,128)(2,1)} %get-tuple-element.50.refs_0_, bf16[2,256,384]{2,1,0:T(8,128)(2,1)} %collective-permute-done.38.refs_1_, bf16[2,256,384]{2,1,0:T(8,128)(2,1)} %collective-permute-done.39.refs_2_, ...), custom_call_target="tpu_custom_call" | custom-call | flops 1811939328 | bytes 6291456 | tf_op jit(solution)/shard_map/pallas_call | solution.py:422
  259.0 3.1 %collective-permute-start.48 = (bf16[3,192,384]{2,1,0:T(8,128)(2,1)S(1)}, bf16[3,192,384]{2,1,0:T(8,128)(2,1)S(1)}, u32[]{:S(2)}, u32[]{:S(2)}) collective-permute-start(bf16[3,192,384]{2,1,0:T(8,128)(2,1)S(1)} %get-tuple-element.60), channel_id=1, source_target_pairs={{0,8},{8,0},{1,9},{9,1},{2,10},{10,2},{3,11},{11,3},{4,12},{12,4},... | collective-permute-start | bytes 1327112 | tf_op jit(solution)/shard_map/ppermute | solution.py:32
  268.2 3.8 %collective-permute-done.31 = bf16[256,384]{1,0:T(8,128)(2,1)S(1)} collective-permute-done((bf16[256,384]{1,0:T(8,128)(2,1)S(1)}, bf16[256,384]{1,0:T(8,128)(2,1)S(1)}, u32[]{:S(2)}, u32[]{:S(2)}) %collective-permute-start.31) | collective-permute-done | bytes 196640 | tf_op jit(solution)/shard_map/ppermute | solution.py:32
  272.4 5.4 %collective-permute-done.48 = bf16[3,192,384]{2,1,0:T(8,128)(2,1)S(1)} collective-permute-done((bf16[3,192,384]{2,1,0:T(8,128)(2,1)S(1)}, bf16[3,192,384]{2,1,0:T(8,128)(2,1)S(1)}, u32[]{:S(2)}, u32[]{:S(2)}) %collective-permute-start.48) | collective-permute-done | bytes 442400 | tf_op jit(solution)/shard_map/ppermute | solution.py:32
  (204 shorter events, 117.3 us)
Async XLA Ops:
  7.7 15.0 %collective-permute-start = (bf16[256,384]{1,0:T(8,128)(2,1)S(1)}, bf16[256,384]{1,0:T(8,128)(2,1)S(1)}, u32[]{:S(2)}, u32[]{:S(2)}) collective-permute-start(bf16[256,384]{1,0:T(8,128)(2,1)S(1)} %fusion.19.refs_0_), channel_id=1, source_target_pairs={{0,1},{1,0},{2,3},{3,2},{4,5},{5,4},{6,7},{7,6},{8,9},{9,8},{10,11... | collective-permute-start | bytes 589832 | tf_op jit(solution)/shard_map/ppermute | solution.py:32
  35.2 52.8 %all-to-all-start = ((bf16[8,2,256,384]{3,2,1,0:T(8,128)(2,1)}), bf16[8,2,256,384]{3,2,1,0:T(8,128)(2,1)S(1)}, u32[]{:S(2)}, u32[]{:S(2)}) async-start(bf16[8,2,256,384]{3,2,1,0:T(8,128)(2,1)} %broadcast_in_dim.16), calls=%async_computation | async-start | bytes 6291456 | tf_op jit(solution)/shard_map/all_to_all | solution.py:465
  100.2 95.8 %all-to-all-start.1 = ((bf16[8,2,256,384]{3,2,1,0:T(8,128)(2,1)}), bf16[8,2,256,384]{3,2,1,0:T(8,128)(2,1)S(1)}, u32[]{:S(2)}, u32[]{:S(2)}) async-start(bf16[8,2,256,384]{3,2,1,0:T(8,128)(2,1)} %get-tuple-element.39), calls=%async_computation.1 | async-start | bytes 6291456 | tf_op jit(solution)/shard_map/all_to_all | solution.py:476
  118.6 15.2 %collective-permute-start.23 = (bf16[256,384]{1,0:T(8,128)(2,1)}, bf16[256,384]{1,0:T(8,128)(2,1)}, u32[]{:S(2)}, u32[]{:S(2)}) collective-permute-start(bf16[256,384]{1,0:T(8,128)(2,1)} %get-tuple-element.71), channel_id=1, source_target_pairs={{0,4},{2,6},{4,0},{6,2},{1,5},{3,7},{5,1},{7,3},{8,12},{10,14},{12... | collective-permute-start | bytes 589832 | tf_op jit(solution)/shard_map/ppermute | solution.py:32
  118.6 15.1 %collective-permute-start.22 = (bf16[256,384]{1,0:T(8,128)(2,1)S(1)}, bf16[256,384]{1,0:T(8,128)(2,1)}, u32[]{:S(2)}, u32[]{:S(2)}) collective-permute-start(bf16[256,384]{1,0:T(8,128)(2,1)S(1)} %get-tuple-element.69), channel_id=1, source_target_pairs={{0,2},{2,0},{4,6},{6,4},{1,3},{3,1},{5,7},{7,5},{8,10},{10,8},{12,... | collective-permute-start | bytes 589832 | tf_op jit(solution)/shard_map/ppermute | solution.py:32
  121.8 36.9 %collective-permute-start.38 = (bf16[2,256,384]{2,1,0:T(8,128)(2,1)}, bf16[2,256,384]{2,1,0:T(8,128)(2,1)}, u32[]{:S(2)}, u32[]{:S(2)}) collective-permute-start(bf16[2,256,384]{2,1,0:T(8,128)(2,1)} %get-tuple-element.51), channel_id=1, source_target_pairs={{0,16},{16,0},{32,48},{48,32},{1,17},{17,1},{33,49},{49,33},{2,18}... | collective-permute-start | bytes 1179656 | tf_op jit(solution)/shard_map/ppermute | solution.py:32
  124.4 44.4 %collective-permute-start.39 = (bf16[2,256,384]{2,1,0:T(8,128)(2,1)}, bf16[2,256,384]{2,1,0:T(8,128)(2,1)}, u32[]{:S(2)}, u32[]{:S(2)}) collective-permute-start(bf16[2,256,384]{2,1,0:T(8,128)(2,1)} %get-tuple-element.52), channel_id=1, source_target_pairs={{0,32},{16,48},{32,0},{48,16},{1,33},{17,49},{33,1},{49,17},{2,34}... | collective-permute-start | bytes 1179656 | tf_op jit(solution)/shard_map/ppermute | solution.py:32
  130.8 39.5 %collective-permute-start.40 = (bf16[2,256,384]{2,1,0:T(8,128)(2,1)}, bf16[2,256,384]{2,1,0:T(8,128)(2,1)}, u32[]{:S(2)}, u32[]{:S(2)}) collective-permute-start(bf16[2,256,384]{2,1,0:T(8,128)(2,1)} %get-tuple-element.53), channel_id=1, source_target_pairs={{0,48},{16,32},{32,16},{48,0},{1,49},{17,33},{33,17},{49,1},{2,50}... | collective-permute-start | bytes 1179656 | tf_op jit(solution)/shard_map/ppermute | solution.py:32
  135.2 35.1 %collective-permute-start.25 = (bf16[256,384]{1,0:T(8,128)(2,1)S(1)}, bf16[256,384]{1,0:T(8,128)(2,1)S(1)}, u32[]{:S(2)}, u32[]{:S(2)}) collective-permute-start(bf16[256,384]{1,0:T(8,128)(2,1)S(1)} %fusion.2), channel_id=1, source_target_pairs={{0,64},{64,0},{1,65},{65,1},{2,66},{66,2},{3,67},{67,3},{4,68},{68... | collective-permute-start | bytes 589832 | tf_op jit(solution)/shard_map/ppermute | solution.py:32
  135.7 36.3 %collective-permute-start.41 = (bf16[2,256,384]{2,1,0:T(8,128)(2,1)}, bf16[2,256,384]{2,1,0:T(8,128)(2,1)}, u32[]{:S(2)}, u32[]{:S(2)}) collective-permute-start(bf16[2,256,384]{2,1,0:T(8,128)(2,1)} %get-tuple-element.50.refs_0_), channel_id=1, source_target_pairs={{0,1},{1,0},{2,3},{3,2},{4,5},{5,4},{6,7},{7,6},{8,9},{9,8},{10,11... | collective-permute-start | bytes 1179656 | tf_op jit(solution)/shard_map/ppermute | solution.py:32
  158.7 15.2 %collective-permute-start.42 = (bf16[2,256,384]{2,1,0:T(8,128)(2,1)}, bf16[2,256,384]{2,1,0:T(8,128)(2,1)}, u32[]{:S(2)}, u32[]{:S(2)}) collective-permute-start(bf16[2,256,384]{2,1,0:T(8,128)(2,1)} %collective-permute-done.38.refs_1_), channel_id=1, source_target_pairs={{0,1},{1,0},{2,3},{3,2},{4,5},{5,4},{6,7},{7,6},{8,9},{9,8},{10,11... | collective-permute-start | bytes 1179656 | tf_op jit(solution)/shard_map/ppermute | solution.py:32
  181.8 38.4 %collective-permute-start.26 = (bf16[4,256,384]{2,1,0:T(8,128)(2,1)}, bf16[4,256,384]{2,1,0:T(8,128)(2,1)}, u32[]{:S(2)}, u32[]{:S(2)}) collective-permute-start(bf16[4,256,384]{2,1,0:T(8,128)(2,1)} %get-tuple-element.42), channel_id=1, source_target_pairs={{0,1},{1,0},{2,3},{3,2},{4,5},{5,4},{6,7},{7,6},{8,9},{9,8},{10,11... | collective-permute-start | bytes 2359304 | tf_op jit(solution)/shard_map/ppermute | solution.py:32
  192.2 20.9 %collective-permute-start.56 = (bf16[192,384]{1,0:T(8,128)(2,1)}, bf16[192,384]{1,0:T(8,128)(2,1)}, u32[]{:S(2)}, u32[]{:S(2)}) collective-permute-start(bf16[192,384]{1,0:T(8,128)(2,1)} %get-tuple-element.75), channel_id=1, source_target_pairs={{0,72},{8,64},{64,8},{72,0},{1,73},{9,65},{65,9},{73,1},{2,74},{10... | collective-permute-start | bytes 442376 | tf_op jit(solution)/shard_map/ppermute | solution.py:32
  193.6 19.6 %collective-permute-start.55 = (bf16[192,384]{1,0:T(8,128)(2,1)}, bf16[192,384]{1,0:T(8,128)(2,1)}, u32[]{:S(2)}, u32[]{:S(2)}) collective-permute-start(bf16[192,384]{1,0:T(8,128)(2,1)} %get-tuple-element.76), channel_id=1, source_target_pairs={{0,64},{64,0},{1,65},{65,1},{2,66},{66,2},{3,67},{67,3},{4,68},{68... | collective-permute-start | bytes 442376 | tf_op jit(solution)/shard_map/ppermute | solution.py:32
  194.5 21.8 %collective-permute-start.54 = (bf16[192,384]{1,0:T(8,128)(2,1)}, bf16[192,384]{1,0:T(8,128)(2,1)}, u32[]{:S(2)}, u32[]{:S(2)}) collective-permute-start(bf16[192,384]{1,0:T(8,128)(2,1)} %get-tuple-element.74), channel_id=1, source_target_pairs={{0,8},{8,0},{1,9},{9,1},{2,10},{10,2},{3,11},{11,3},{4,12},{12,4},... | collective-permute-start | bytes 442376 | tf_op jit(solution)/shard_map/ppermute | solution.py:32
  213.1 14.7 %collective-permute-start.45 = (bf16[3,256,384]{2,1,0:T(8,128)(2,1)S(1)}, bf16[3,256,384]{2,1,0:T(8,128)(2,1)S(1)}, u32[]{:S(2)}, u32[]{:S(2)}) collective-permute-start(bf16[3,256,384]{2,1,0:T(8,128)(2,1)S(1)} %copy-done), channel_id=1, source_target_pairs={{0,16},{16,0},{32,48},{48,32},{1,17},{17,1},{33,49},{49,33},{2,18}... | collective-permute-start | bytes 1769480 | tf_op jit(solution)/shard_map/ppermute | solution.py:32
  213.2 28.9 %collective-permute-start.46 = (bf16[3,256,384]{2,1,0:T(8,128)(2,1)S(1)}, bf16[3,256,384]{2,1,0:T(8,128)(2,1)S(1)}, u32[]{:S(2)}, u32[]{:S(2)}) collective-permute-start(bf16[3,256,384]{2,1,0:T(8,128)(2,1)S(1)} %copy-done), channel_id=1, source_target_pairs={{0,32},{16,48},{32,0},{48,16},{1,33},{17,49},{33,1},{49,17},{2,34}... | collective-permute-start | bytes 1769480 | tf_op jit(solution)/shard_map/ppermute | solution.py:32
  216.3 27.9 %collective-permute-start.47 = (bf16[3,256,384]{2,1,0:T(8,128)(2,1)S(1)}, bf16[3,256,384]{2,1,0:T(8,128)(2,1)}, u32[]{:S(2)}, u32[]{:S(2)}) collective-permute-start(bf16[3,256,384]{2,1,0:T(8,128)(2,1)S(1)} %copy-done), channel_id=1, source_target_pairs={{0,48},{16,32},{32,16},{48,0},{1,49},{17,33},{33,17},{49,1},{2,50}... | collective-permute-start | bytes 1769480 | tf_op jit(solution)/shard_map/ppermute | solution.py:32
  217.0 36.1 %collective-permute-start.30 = (bf16[4,256,384]{2,1,0:T(8,128)(2,1)}, bf16[4,256,384]{2,1,0:T(8,128)(2,1)S(1)}, u32[]{:S(2)}, u32[]{:S(2)}) collective-permute-start(bf16[4,256,384]{2,1,0:T(8,128)(2,1)} %get-tuple-element.48), channel_id=1, source_target_pairs={{0,1},{1,0},{2,3},{3,2},{4,5},{5,4},{6,7},{7,6},{8,9},{9,8},{10,11... | collective-permute-start | bytes 2359304 | tf_op jit(solution)/shard_map/ppermute | solution.py:32
  224.3 33.4 %collective-permute-start.29 = (bf16[256,384]{1,0:T(8,128)(2,1)}, bf16[256,384]{1,0:T(8,128)(2,1)}, u32[]{:S(2)}, u32[]{:S(2)}) collective-permute-start(bf16[256,384]{1,0:T(8,128)(2,1)} %get-tuple-element.67), channel_id=1, source_target_pairs={{0,6},{2,4},{4,2},{6,0},{1,7},{3,5},{5,3},{7,1},{8,14},{10,12},{12... | collective-permute-start | bytes 589832 | tf_op jit(solution)/shard_map/ppermute | solution.py:32
  227.8 31.2 %collective-permute-start.28 = (bf16[256,384]{1,0:T(8,128)(2,1)}, bf16[256,384]{1,0:T(8,128)(2,1)}, u32[]{:S(2)}, u32[]{:S(2)}) collective-permute-start(bf16[256,384]{1,0:T(8,128)(2,1)} %get-tuple-element.68), channel_id=1, source_target_pairs={{0,4},{2,6},{4,0},{6,2},{1,5},{3,7},{5,1},{7,3},{8,12},{10,14},{12... | collective-permute-start | bytes 589832 | tf_op jit(solution)/shard_map/ppermute | solution.py:32
  242.9 19.2 %collective-permute-start.27 = (bf16[256,384]{1,0:T(8,128)(2,1)S(1)}, bf16[256,384]{1,0:T(8,128)(2,1)}, u32[]{:S(2)}, u32[]{:S(2)}) collective-permute-start(bf16[256,384]{1,0:T(8,128)(2,1)S(1)} %get-tuple-element.66), channel_id=1, source_target_pairs={{0,2},{2,0},{4,6},{6,4},{1,3},{3,1},{5,7},{7,5},{8,10},{10,8},{12,... | collective-permute-start | bytes 589832 | tf_op jit(solution)/shard_map/ppermute | solution.py:32
  254.8 17.6 %collective-permute-start.50 = (bf16[3,192,384]{2,1,0:T(8,128)(2,1)S(1)}, bf16[3,192,384]{2,1,0:T(8,128)(2,1)S(1)}, u32[]{:S(2)}, u32[]{:S(2)}) collective-permute-start(bf16[3,192,384]{2,1,0:T(8,128)(2,1)S(1)} %get-tuple-element.61), channel_id=1, source_target_pairs={{0,72},{8,64},{1,73},{9,65},{2,74},{10,66},{3,75},{11,67},{4,76},{... | collective-permute-start | bytes 1327112 | tf_op jit(solution)/shard_map/ppermute | solution.py:32
  259.0 18.8 %collective-permute-start.48 = (bf16[3,192,384]{2,1,0:T(8,128)(2,1)S(1)}, bf16[3,192,384]{2,1,0:T(8,128)(2,1)S(1)}, u32[]{:S(2)}, u32[]{:S(2)}) collective-permute-start(bf16[3,192,384]{2,1,0:T(8,128)(2,1)S(1)} %get-tuple-element.60), channel_id=1, source_target_pairs={{0,8},{8,0},{1,9},{9,1},{2,10},{10,2},{3,11},{11,3},{4,12},{12,4},... | collective-permute-start | bytes 1327112 | tf_op jit(solution)/shard_map/ppermute | solution.py:32
  (72 other events, 574.7 us)
where the time goes:
time: 286 us; the launch traced here: 281 us
  starting transfers between devices  93.8 us (33%)
  waiting for transfers between devices  83.5 us (29%)
  Pallas kernels  65.9 us (23%)
  other arithmetic  20.6 us (7%)
  local copies, waits for them, and re-layouts  15.3 us (5%)
    ppermute x57, waiting for transfers between devices, moved(): return lax.ppermute(array, axis, pairs)  83.5 us
    ppermute x57, starting transfers between devices, moved(): return lax.ppermute(array, axis, pairs)  80.4 us
    pallas_call x6, Pallas kernels, run(): pl.pallas_call(body, grid_spec=pltpu.PrefetchScalarGridSpec(num_scalar_pr...  41.7 us
    pallas_call x2, Pallas kernels, token_sum(): pl.pallas_call(token_sum_kernel, grid_spec=pltpu.PrefetchScalarGridSpec(n...  13.8 us
    pallas_call x1, Pallas kernels, attention(): pl.pallas_call(functools.partial(attention_kernel, HD ** (-0.5)), grid=(h...  10.5 us
    unnamed x75, local copies, waits for them, and re-layouts  7.07 us
    all_to_all x1, starting transfers between devices, on_device(): lax.all_to_all(jnp.broadcast_to(qkv[1:], (8, 2, tok, width)), ROW, split_...  6.78 us
    all_to_all x1, starting transfers between devices, on_device(): dkv_all = lax.all_to_all(dkv, ROW, split_axis=0, concat_axis=0, tiled=True)  6.56 us
  transfers between devices with their start and end apart: 59, of which 23 were waited for; matrix products, arithmetic and copies ran while one was open for 9% of the time, Pallas kernels for 17%

commit v1 on v0

--- a/solution.py
+++ b/solution.py
@@ -92,8 +92,8 @@
 
 def norm_qkv_kernel(place, *refs):
     pieces, (mods, w) = refs[:8], refs[8:10]
-    cols, qkv, stats = refs[10:13]
-    whole, wbuf, sems = refs[13:]
+    cols, q_out, kv_out, stats = refs[10:14]
+    whole, wbuf, sems = refs[14:]
     tok, width = pieces[0].shape
 
     def fetch(c):
@@ -134,7 +134,15 @@
     @pl.loop(0, 3)
     def _(c):
         fetch(c).wait()
-        qkv[c] = dot_nn(whole[...], wbuf[c]).astype(BF16)
+        part = dot_nn(whole[...], wbuf[c]).astype(BF16)
+
+        @pl.when(c == 0)
+        def _():
+            q_out[...] = part
+
+        @pl.when(c > 0)
+        def _():
+            kv_out[jnp.maximum(c - 1, 0)] = part
 
 
 def norm_qkv(place, pieces, mods, w):
@@ -144,7 +152,12 @@
         place,
         (*pieces, mods, w),
         [full((tok, width))] * 8 + [full(mods.shape), ANY],
-        [shaped((4, tok, width)), shaped((3, tok, width)), shaped((2, tok, 128), F32)],
+        [
+            shaped((4, tok, width)),
+            shaped((tok, width)),
+            shaped((2, tok, width)),
+            shaped((2, tok, 128), F32),
+        ],
         [
             pltpu.VMEM((tok, 8 * width), BF16),
             pltpu.VMEM(w.shape, BF16),
@@ -332,7 +345,7 @@
 
 
 def attention_kernel(scaling, q_ref, g_ref, k_ref, v_ref, o_ref, dq_ref, dkv_ref, scores):
-    q, g = q_ref[0], g_ref[...]
+    q, g = q_ref[...], g_ref[...]
     blocks, _, tok, _ = k_ref.shape
     peak = None
     for b in range(blocks):
@@ -362,7 +375,7 @@
     dq_ref[...] = (jnp.transpose(dq) * scaling).astype(BF16)
 
 
-def attention(qkv, grad, kv):
+def attention(query, grad, kv):
     tok, width = grad.shape
     heads, blocks = width // HD, kv.shape[0]
     one = pl.BlockSpec((tok, HD), lambda j: (0, j))
@@ -370,7 +383,7 @@
         functools.partial(attention_kernel, HD**-0.5),
         grid=(heads,),
         in_specs=[
-            pl.BlockSpec((1, tok, HD), lambda j: (0, 0, j)),
+            one,
             one,
             pl.BlockSpec((blocks, 1, tok, HD), lambda j: (0, 0, 0, j)),
             pl.BlockSpec((blocks, 1, tok, HD), lambda j: (0, 1, 0, j)),
@@ -383,7 +396,7 @@
         ],
         scratch_shapes=[pltpu.VMEM((blocks, tok, tok), F32)],
         cost_estimate=cost(12 * tok * blocks * tok * width, 8 * 2**20, tok * blocks * tok * heads),
-    )(qkv, grad, kv, kv)
+    )(query, grad, kv, kv)
 
 
 def token_sum_kernel(place, *refs):
@@ -461,9 +474,9 @@
     whole = gather_head(inputs)
     cot_late = lax.optimization_barrier((cotangent, whole[2], whole[4], whole[6]))[0]
     cot_full = gather_head(cot_late)
-    ncols, qkv, stats = norm_qkv(place, whole, chosen, w_qkv)
+    ncols, query, kv, stats = norm_qkv(place, whole, chosen, w_qkv)
     kv_full = lax.all_to_all(
-        jnp.broadcast_to(qkv[1:], (8, 2, tok, width)), ROW, split_axis=0, concat_axis=0, tiled=True
+        jnp.broadcast_to(kv, (8, *kv.shape)), ROW, split_axis=0, concat_axis=0, tiled=True
     )
 
     incoming, gated, ccols = hint_back(place, cot_full, chosen, zero_weight)
@@ -472,7 +485,7 @@
     cols = packs[:1] + [swap(packs[d], "row_0", 4, d) for d in (1, 2, 3)]
     cols_other = [swap(a, "core", 2, 1) for a in cols]
 
-    attn, dquery, dkv = attention(qkv, attn_grad, kv_full)
+    attn, dquery, dkv = attention(query, attn_grad, kv_full)
     dkv_all = lax.all_to_all(dkv, ROW, split_axis=0, concat_axis=0, tiled=True)
 
     branch = sum_head(*spread(place, attn, w_out))

time: 286 us -> 279 us (0.976)
  starting transfers between devices: 93.8 us -> 84.1 us
  waiting for transfers between devices: 83.5 us -> 88.1 us
    ppermute x57, starting transfers between devices: 80.4 us -> 72.6 us  [moved(): return lax.ppermute(array, axis, pairs)]
  transfers between devices with their start and end apart: 59 -> 59, of which waited for: 23 -> 19; matrix products, arithmetic and copies ran while one was open for 9% -> 9% of each run, Pallas kernels for 17% -> 17%
where the time goes in v1:
time: 279 us; the launch traced here: 276 us
  waiting for transfers between devices  88.1 us (32%)
  starting transfers between devices  84.1 us (30%)
  Pallas kernels  66.2 us (24%)
  other arithmetic  20.6 us (7%)
  local copies, waits for them, and re-layouts  14.8 us (5%)
    ppermute x57, waiting for transfers between devices, moved(): return lax.ppermute(array, axis, pairs)  85.4 us
    ppermute x57, starting transfers between devices, moved(): return lax.ppermute(array, axis, pairs)  72.6 us
    pallas_call x6, Pallas kernels, run(): pl.pallas_call(body, grid_spec=pltpu.PrefetchScalarGridSpec(num_scalar_pr...  41.9 us
    pallas_call x2, Pallas kernels, token_sum(): pl.pallas_call(token_sum_kernel, grid_spec=pltpu.PrefetchScalarGridSpec(n...  13.8 us
    pallas_call x1, Pallas kernels, attention(): pl.pallas_call(functools.partial(attention_kernel, HD ** (-0.5)), grid=(h...  10.5 us
    all_to_all x1, starting transfers between devices, on_device(): lax.all_to_all(jnp.broadcast_to(kv, (8, *kv.shape)), ROW, split_axis=0, c...  6.78 us
    unnamed x75, local copies, waits for them, and re-layouts  6.62 us
  transfers between devices with their start and end apart: 59, of which 19 were waited for; matrix products, arithmetic and copies ran while one was open for 9% of the time, Pallas kernels for 17%

profile of v1, /device:TPU:1, one launch (start us, length us, event | category | flops | bytes accessed | tf_op | source)
XLA Modules:
  0.0 275.6 jit_solution(7586716084867040327)
XLA Ops:
  1.8 4.7 %collective-permute-start.5 = (bf16[256,384]{1,0:T(8,128)(2,1)S(1)}, bf16[256,384]{1,0:T(8,128)(2,1)S(1)}, u32[]{:S(2)}, u32[]{:S(2)}) collective-permute-start(bf16[256,384]{1,0:T(8,128)(2,1)S(1)} %fusion.19.refs_0_), channel_id=1, source_target_pairs={{0,6},{2,4},{4,2},{6,0},{1,7},{3,5},{5,3},{7,1},{8,14},{10,12},{12... | collective-permute-start | bytes 589832 | tf_op jit(solution)/shard_map/ppermute | solution.py:32
  9.1 5.9 %collective-permute-done.5.refs_6_ = bf16[256,384]{1,0:T(8,128)(2,1)S(1)} collective-permute-done((bf16[256,384]{1,0:T(8,128)(2,1)S(1)}, bf16[256,384]{1,0:T(8,128)(2,1)S(1)}, u32[]{:S(2)}, u32[]{:S(2)}) %collective-permute-start.5) | collective-permute-done | bytes 196640 | tf_op jit(solution)/shard_map/ppermute | solution.py:32
  20.5 8.8 %shard_map.127 = (bf16[4,256,384]{2,1,0:T(8,128)(2,1)}, bf16[256,384]{1,0:T(8,128)(2,1)}, bf16[2,256,384]{2,1,0:T(8,128)(2,1)}, f32[2,256,128]{2,1,0:T(8,128)}) custom-call(s32[6]{0:T(128)} %stack.27.place, bf16[256,384]{1,0:T(8,128)(2,1)} %copy-done.1, bf16[256,384]{1,0:T(8,128)(2,1)} %copy-done.15, bf16[256,384]{1,0:T(8,128)(2,1)} %copy-done.14, ...), custom_call_target="tpu_custom_call" | custom-call | flops 1811939328 | bytes 12582912 | tf_op jit(solution)/shard_map/pallas_call | solution.py:52
  29.2 3.1 %broadcast_in_dim.16 = bf16[8,2,256,384]{3,2,1,0:T(8,128)(2,1)} broadcast(bf16[2,256,384]{2,1,0:T(8,128)(2,1)} %get-tuple-element.37), dimensions={1,2,3} | broadcast | bytes 3538944 | tf_op jit(solution)/shard_map/broadcast_in_dim | solution.py:479
  32.4 6.8 %all-to-all-start = ((bf16[8,2,256,384]{3,2,1,0:T(8,128)(2,1)}), bf16[8,2,256,384]{3,2,1,0:T(8,128)(2,1)S(1)}, u32[]{:S(2)}, u32[]{:S(2)}) async-start(bf16[8,2,256,384]{3,2,1,0:T(8,128)(2,1)} %broadcast_in_dim.16), calls=%async_computation | async-start | bytes 6291456 | tf_op jit(solution)/shard_map/all_to_all | solution.py:478
  43.7 6.6 %collective-permute-done.12.refs_6_ = bf16[256,384]{1,0:T(8,128)(2,1)S(1)} collective-permute-done((bf16[256,384]{1,0:T(8,128)(2,1)S(1)}, bf16[256,384]{1,0:T(8,128)(2,1)S(1)}, u32[]{:S(2)}, u32[]{:S(2)}) %collective-permute-start.12) | collective-permute-done | bytes 196640 | tf_op jit(solution)/shard_map/ppermute | solution.py:32
  54.4 5.8 %shard_map.128 = (bf16[256,384]{1,0:T(8,128)(2,1)}, bf16[256,384]{1,0:T(8,128)(2,1)}, bf16[4,256,384]{2,1,0:T(8,128)(2,1)}) custom-call(s32[6]{0:T(128)} %stack.27.place, bf16[256,384]{1,0:T(8,128)(2,1)} %refs_0_, bf16[256,384]{1,0:T(8,128)(2,1)} %copy-done.29, bf16[256,384]{1,0:T(8,128)(2,1)} %copy-done.28, ...), custom_call_target="tpu_custom_call" | custom-call | flops 603979776 | bytes 6291456 | tf_op jit(solution)/shard_map/pallas_call | solution.py:52
  64.8 6.9 %collective-permute-done.19.refs_6_ = bf16[256,384]{1,0:T(8,128)(2,1)S(1)} collective-permute-done((bf16[256,384]{1,0:T(8,128)(2,1)}, bf16[256,384]{1,0:T(8,128)(2,1)S(1)}, u32[]{:S(2)}, u32[]{:S(2)}) %collective-permute-start.19) | collective-permute-done | bytes 196640 | tf_op jit(solution)/shard_map/ppermute | solution.py:32
  75.7 6.0 %shard_map.129 = (bf16[256,384]{1,0:T(8,128)(2,1)}, bf16[2,256,384]{2,1,0:T(8,128)(2,1)}, bf16[2,256,384]{2,1,0:T(8,128)(2,1)}, bf16[2,256,384]{2,1,0:T(8,128)(2,1)}, bf16[2,256,384]{2,1,0:T(8,128)(2,1)}) custom-call(s32[6]{0:T(128)} %stack.27.place, bf16[256,384]{1,0:T(8,128)(2,1)} %get-tuple-element.33.refs_0_, bf16[256,384]{1,0:T(8,128)(2,1)} %copy-done.27, ...), custom_call_target="tpu_custom_call" | custom-call | flops 603979776 | bytes 8388608 | tf_op jit(solution)/shard_map/pallas_call | solution.py:52
  86.1 10.5 %shard_map.130 = (bf16[256,384]{1,0:T(8,128)(2,1)}, bf16[256,384]{1,0:T(8,128)(2,1)}, bf16[8,2,256,384]{3,2,1,0:T(8,128)(2,1)}) custom-call(bf16[256,384]{1,0:T(8,128)(2,1)} %get-tuple-element.31.q_ref, bf16[256,384]{1,0:T(8,128)(2,1)} %get-tuple-element.36.g_ref, bf16[8,2,256,384]{3,2,1,0:T(8,128)(2,1)} %copy-done.4, bf16[8,2,256,384]{3,2,1,0:T(8,128)(2,1)} %copy-done.4), custom_call_target="tpu_custom_call" | custom-call | flops 2415919104 | bytes 8388608 | tf_op jit(solution)/shard_map/pallas_call | solution.py:382
  96.6 4.8 %all-to-all-start.1 = ((bf16[8,2,256,384]{3,2,1,0:T(8,128)(2,1)}), bf16[8,2,256,384]{3,2,1,0:T(8,128)(2,1)S(1)}, u32[]{:S(2)}, u32[]{:S(2)}) async-start(bf16[8,2,256,384]{3,2,1,0:T(8,128)(2,1)} %get-tuple-element.41), calls=%async_computation.1 | async-start | bytes 6291456 | tf_op jit(solution)/shard_map/all_to_all | solution.py:489
  101.4 6.0 %shard_map.131 = (bf16[4,256,384]{2,1,0:T(8,128)(2,1)}, bf16[4,256,384]{2,1,0:T(8,128)(2,1)}) custom-call(s32[6]{0:T(128)} %stack.27.place, bf16[256,384]{1,0:T(8,128)(2,1)} %get-tuple-element.38.a, bf16[3072,384]{1,0:T(8,128)(2,1)} %bitcast.103), custom_call_target="tpu_custom_call" | custom-call | flops 603979776 | bytes 6291456 | tf_op jit(solution)/shard_map/pallas_call | solution.py:52
  123.3 3.5 %collective-permute-done.23 = bf16[256,384]{1,0:T(8,128)(2,1)} collective-permute-done((bf16[256,384]{1,0:T(8,128)(2,1)S(1)}, bf16[256,384]{1,0:T(8,128)(2,1)}, u32[]{:S(2)}, u32[]{:S(2)}) %collective-permute-start.23) | collective-permute-done | bytes 196640 | tf_op jit(solution)/shard_map/ppermute | solution.py:32
  130.3 21.2 %collective-permute-done.38.refs_1_ = bf16[2,256,384]{2,1,0:T(8,128)(2,1)} collective-permute-done((bf16[2,256,384]{2,1,0:T(8,128)(2,1)}, bf16[2,256,384]{2,1,0:T(8,128)(2,1)}, u32[]{:S(2)}, u32[]{:S(2)}) %collective-permute-start.38) | collective-permute-done | bytes 393248 | tf_op jit(solution)/shard_map/ppermute | solution.py:32
  151.4 4.2 %collective-permute-start.42 = (bf16[2,256,384]{2,1,0:T(8,128)(2,1)}, bf16[2,256,384]{2,1,0:T(8,128)(2,1)}, u32[]{:S(2)}, u32[]{:S(2)}) collective-permute-start(bf16[2,256,384]{2,1,0:T(8,128)(2,1)} %collective-permute-done.38.refs_1_), channel_id=1, source_target_pairs={{0,1},{1,0},{2,3},{3,2},{4,5},{5,4},{6,7},{7,6},{8,9},{9,8},{10,11... | collective-permute-start | bytes 1179656 | tf_op jit(solution)/shard_map/ppermute | solution.py:32
  155.6 7.3 %collective-permute-done.39.refs_2_ = bf16[2,256,384]{2,1,0:T(8,128)(2,1)} collective-permute-done((bf16[2,256,384]{2,1,0:T(8,128)(2,1)}, bf16[2,256,384]{2,1,0:T(8,128)(2,1)}, u32[]{:S(2)}, u32[]{:S(2)}) %collective-permute-start.39) | collective-permute-done | bytes 393248 | tf_op jit(solution)/shard_map/ppermute | solution.py:32
  169.8 5.9 %shard_map.132 = (bf16[4,256,384]{2,1,0:T(8,128)(2,1)}, bf16[4,256,384]{2,1,0:T(8,128)(2,1)}) custom-call(s32[6]{0:T(128)} %stack.27.place, bf16[256,384]{1,0:T(8,128)(2,1)} %get-tuple-element.61.a, bf16[3072,384]{1,0:T(8,128)(2,1)} %w.1), custom_call_target="tpu_custom_call" | custom-call | flops 603979776 | bytes 6291456 | tf_op jit(solution)/shard_map/pallas_call | solution.py:52
  178.5 4.9 %shard_map.135 = bf16[2,2,1,192,384]{4,3,2,1,0:T(8,128)(2,1)} custom-call(s32[6]{0:T(128)} %stack.27.place, bf16[2,256,384]{2,1,0:T(8,128)(2,1)} %get-tuple-element.52.refs_0_, bf16[2,256,384]{2,1,0:T(8,128)(2,1)} %collective-permute-done.38.refs_1_, bf16[2,256,384]{2,1,0:T(8,128)(2,1)} %collective-permute-done.39.refs_2_, ...), custom_call_target="tpu_custom_call" | custom-call | flops 603979776 | bytes 6291456 | tf_op jit(solution)/shard_map/pallas_call | solution.py:435
  191.3 9.5 %shard_map.133 = (bf16[4,256,384]{2,1,0:T(8,128)(2,1)}, bf16[4,256,384]{2,1,0:T(8,128)(2,1)}, f32[8,256]{1,0:T(8,128)}) custom-call(s32[6]{0:T(128)} %stack.27.place, bf16[3,256,384]{2,1,0:T(8,128)(2,1)} %pad_maximum_fusion.grads.refs_8_, bf16[3,3072,384]{2,1,0:T(8,128)(2,1)} %bitcast.101, f32[3,3072]{1,0:T(4,128)} %bitcast.106, ...), custom_call_target="tpu_custom_call" | custom-call | flops 1811939328 | bytes 14680064 | tf_op jit(solution)/shard_map/pallas_call | solution.py:52
  217.8 16.8 %collective-permute-done.47.refs_11_ = bf16[3,256,384]{2,1,0:T(8,128)(2,1)S(1)} collective-permute-done((bf16[3,256,384]{2,1,0:T(8,128)(2,1)S(1)}, bf16[3,256,384]{2,1,0:T(8,128)(2,1)S(1)}, u32[]{:S(2)}, u32[]{:S(2)}) %collective-permute-start.47) | collective-permute-done | bytes 589856 | tf_op jit(solution)/shard_map/ppermute | solution.py:32
  239.2 8.8 %shard_map.134 = bf16[2,2,3,192,384]{4,3,2,1,0:T(8,128)(2,1)} custom-call(s32[6]{0:T(128)} %stack.27.place, bf16[2,256,384]{2,1,0:T(8,128)(2,1)} %get-tuple-element.52.refs_0_, bf16[2,256,384]{2,1,0:T(8,128)(2,1)} %collective-permute-done.38.refs_1_, bf16[2,256,384]{2,1,0:T(8,128)(2,1)} %collective-permute-done.39.refs_2_, ...), custom_call_target="tpu_custom_call" | custom-call | flops 1811939328 | bytes 6291456 | tf_op jit(solution)/shard_map/pallas_call | solution.py:435
  249.8 3.5 %collective-permute-start.48 = (bf16[3,192,384]{2,1,0:T(8,128)(2,1)S(1)}, bf16[3,192,384]{2,1,0:T(8,128)(2,1)S(1)}, u32[]{:S(2)}, u32[]{:S(2)}) collective-permute-start(bf16[3,192,384]{2,1,0:T(8,128)(2,1)S(1)} %get-tuple-element.62), channel_id=1, source_target_pairs={{0,8},{8,0},{1,9},{9,1},{2,10},{10,2},{3,11},{11,3},{4,12},{12,4},... | collective-permute-start | bytes 1327112 | tf_op jit(solution)/shard_map/ppermute | solution.py:32
  261.4 3.1 %collective-permute-done.33 = bf16[256,384]{1,0:T(8,128)(2,1)S(1)} collective-permute-done((bf16[256,384]{1,0:T(8,128)(2,1)S(1)}, bf16[256,384]{1,0:T(8,128)(2,1)S(1)}, u32[]{:S(2)}, u32[]{:S(2)}) %collective-permute-start.33) | collective-permute-done | bytes 196640 | tf_op jit(solution)/shard_map/ppermute | solution.py:32
  265.0 5.6 %collective-permute-done.49 = bf16[3,192,384]{2,1,0:T(8,128)(2,1)S(1)} collective-permute-done((bf16[3,192,384]{2,1,0:T(8,128)(2,1)S(1)}, bf16[3,192,384]{2,1,0:T(8,128)(2,1)S(1)}, u32[]{:S(2)}, u32[]{:S(2)}) %collective-permute-start.49) | collective-permute-done | bytes 442400 | tf_op jit(solution)/shard_map/ppermute | solution.py:32
  (203 shorter events, 103.7 us)
Async XLA Ops:
  1.8 13.1 %collective-permute-start.5 = (bf16[256,384]{1,0:T(8,128)(2,1)S(1)}, bf16[256,384]{1,0:T(8,128)(2,1)S(1)}, u32[]{:S(2)}, u32[]{:S(2)}) collective-permute-start(bf16[256,384]{1,0:T(8,128)(2,1)S(1)} %fusion.19.refs_0_), channel_id=1, source_target_pairs={{0,6},{2,4},{4,2},{6,0},{1,7},{3,5},{5,3},{7,1},{8,14},{10,12},{12... | collective-permute-start | bytes 589832 | tf_op jit(solution)/shard_map/ppermute | solution.py:32
  32.4 52.0 %all-to-all-start = ((bf16[8,2,256,384]{3,2,1,0:T(8,128)(2,1)}), bf16[8,2,256,384]{3,2,1,0:T(8,128)(2,1)S(1)}, u32[]{:S(2)}, u32[]{:S(2)}) async-start(bf16[8,2,256,384]{3,2,1,0:T(8,128)(2,1)} %broadcast_in_dim.16), calls=%async_computation | async-start | bytes 6291456 | tf_op jit(solution)/shard_map/all_to_all | solution.py:478
  96.6 91.4 %all-to-all-start.1 = ((bf16[8,2,256,384]{3,2,1,0:T(8,128)(2,1)}), bf16[8,2,256,384]{3,2,1,0:T(8,128)(2,1)S(1)}, u32[]{:S(2)}, u32[]{:S(2)}) async-start(bf16[8,2,256,384]{3,2,1,0:T(8,128)(2,1)} %get-tuple-element.41), calls=%async_computation.1 | async-start | bytes 6291456 | tf_op jit(solution)/shard_map/all_to_all | solution.py:489
  117.7 33.7 %collective-permute-start.38 = (bf16[2,256,384]{2,1,0:T(8,128)(2,1)}, bf16[2,256,384]{2,1,0:T(8,128)(2,1)}, u32[]{:S(2)}, u32[]{:S(2)}) collective-permute-start(bf16[2,256,384]{2,1,0:T(8,128)(2,1)} %get-tuple-element.53), channel_id=1, source_target_pairs={{0,16},{16,0},{32,48},{48,32},{1,17},{17,1},{33,49},{49,33},{2,18}... | collective-permute-start | bytes 1179656 | tf_op jit(solution)/shard_map/ppermute | solution.py:32
  120.3 42.7 %collective-permute-start.39 = (bf16[2,256,384]{2,1,0:T(8,128)(2,1)}, bf16[2,256,384]{2,1,0:T(8,128)(2,1)}, u32[]{:S(2)}, u32[]{:S(2)}) collective-permute-start(bf16[2,256,384]{2,1,0:T(8,128)(2,1)} %get-tuple-element.54), channel_id=1, source_target_pairs={{0,32},{16,48},{32,0},{48,16},{1,33},{17,49},{33,1},{49,17},{2,34}... | collective-permute-start | bytes 1179656 | tf_op jit(solution)/shard_map/ppermute | solution.py:32
  122.7 42.0 %collective-permute-start.40 = (bf16[2,256,384]{2,1,0:T(8,128)(2,1)}, bf16[2,256,384]{2,1,0:T(8,128)(2,1)}, u32[]{:S(2)}, u32[]{:S(2)}) collective-permute-start(bf16[2,256,384]{2,1,0:T(8,128)(2,1)} %get-tuple-element.55), channel_id=1, source_target_pairs={{0,48},{16,32},{32,16},{48,0},{1,49},{17,33},{33,17},{49,1},{2,50}... | collective-permute-start | bytes 1179656 | tf_op jit(solution)/shard_map/ppermute | solution.py:32
  128.3 36.5 %collective-permute-start.25 = (bf16[256,384]{1,0:T(8,128)(2,1)S(1)}, bf16[256,384]{1,0:T(8,128)(2,1)S(1)}, u32[]{:S(2)}, u32[]{:S(2)}) collective-permute-start(bf16[256,384]{1,0:T(8,128)(2,1)S(1)} %fusion.2), channel_id=1, source_target_pairs={{0,64},{64,0},{1,65},{65,1},{2,66},{66,2},{3,67},{67,3},{4,68},{68... | collective-permute-start | bytes 589832 | tf_op jit(solution)/shard_map/ppermute | solution.py:32
  128.8 37.8 %collective-permute-start.41 = (bf16[2,256,384]{2,1,0:T(8,128)(2,1)}, bf16[2,256,384]{2,1,0:T(8,128)(2,1)}, u32[]{:S(2)}, u32[]{:S(2)}) collective-permute-start(bf16[2,256,384]{2,1,0:T(8,128)(2,1)} %get-tuple-element.52.refs_0_), channel_id=1, source_target_pairs={{0,1},{1,0},{2,3},{3,2},{4,5},{5,4},{6,7},{7,6},{8,9},{9,8},{10,11... | collective-permute-start | bytes 1179656 | tf_op jit(solution)/shard_map/ppermute | solution.py:32
  151.4 15.4 %collective-permute-start.42 = (bf16[2,256,384]{2,1,0:T(8,128)(2,1)}, bf16[2,256,384]{2,1,0:T(8,128)(2,1)}, u32[]{:S(2)}, u32[]{:S(2)}) collective-permute-start(bf16[2,256,384]{2,1,0:T(8,128)(2,1)} %collective-permute-done.38.refs_1_), channel_id=1, source_target_pairs={{0,1},{1,0},{2,3},{3,2},{4,5},{5,4},{6,7},{7,6},{8,9},{9,8},{10,11... | collective-permute-start | bytes 1179656 | tf_op jit(solution)/shard_map/ppermute | solution.py:32
  163.0 12.7 %collective-permute-start.43 = (bf16[2,256,384]{2,1,0:T(8,128)(2,1)}, bf16[2,256,384]{2,1,0:T(8,128)(2,1)}, u32[]{:S(2)}, u32[]{:S(2)}) collective-permute-start(bf16[2,256,384]{2,1,0:T(8,128)(2,1)} %collective-permute-done.39.refs_2_), channel_id=1, source_target_pairs={{0,1},{1,0},{2,3},{3,2},{4,5},{5,4},{6,7},{7,6},{8,9},{9,8},{10,11... | collective-permute-start | bytes 1179656 | tf_op jit(solution)/shard_map/ppermute | solution.py:32
  164.8 12.5 %collective-permute-start.44 = (bf16[2,256,384]{2,1,0:T(8,128)(2,1)}, bf16[2,256,384]{2,1,0:T(8,128)(2,1)}, u32[]{:S(2)}, u32[]{:S(2)}) collective-permute-start(bf16[2,256,384]{2,1,0:T(8,128)(2,1)} %collective-permute-done.40.refs_3_), channel_id=1, source_target_pairs={{0,1},{1,0},{2,3},{3,2},{4,5},{5,4},{6,7},{7,6},{8,9},{9,8},{10,11... | collective-permute-start | bytes 1179656 | tf_op jit(solution)/shard_map/ppermute | solution.py:32
  175.7 37.0 %collective-permute-start.26 = (bf16[4,256,384]{2,1,0:T(8,128)(2,1)}, bf16[4,256,384]{2,1,0:T(8,128)(2,1)}, u32[]{:S(2)}, u32[]{:S(2)}) collective-permute-start(bf16[4,256,384]{2,1,0:T(8,128)(2,1)} %get-tuple-element.44), channel_id=1, source_target_pairs={{0,1},{1,0},{2,3},{3,2},{4,5},{5,4},{6,7},{7,6},{8,9},{9,8},{10,11... | collective-permute-start | bytes 2359304 | tf_op jit(solution)/shard_map/ppermute | solution.py:32
  185.3 20.5 %collective-permute-start.54 = (bf16[192,384]{1,0:T(8,128)(2,1)}, bf16[192,384]{1,0:T(8,128)(2,1)}, u32[]{:S(2)}, u32[]{:S(2)}) collective-permute-start(bf16[192,384]{1,0:T(8,128)(2,1)} %get-tuple-element.76), channel_id=1, source_target_pairs={{0,8},{8,0},{1,9},{9,1},{2,10},{10,2},{3,11},{11,3},{4,12},{12,4},... | collective-permute-start | bytes 442376 | tf_op jit(solution)/shard_map/ppermute | solution.py:32
  186.3 19.7 %collective-permute-start.56 = (bf16[192,384]{1,0:T(8,128)(2,1)}, bf16[192,384]{1,0:T(8,128)(2,1)}, u32[]{:S(2)}, u32[]{:S(2)}) collective-permute-start(bf16[192,384]{1,0:T(8,128)(2,1)} %get-tuple-element.77), channel_id=1, source_target_pairs={{0,72},{8,64},{64,8},{72,0},{1,73},{9,65},{65,9},{73,1},{2,74},{10... | collective-permute-start | bytes 442376 | tf_op jit(solution)/shard_map/ppermute | solution.py:32
  187.1 19.8 %collective-permute-start.55 = (bf16[192,384]{1,0:T(8,128)(2,1)}, bf16[192,384]{1,0:T(8,128)(2,1)}, u32[]{:S(2)}, u32[]{:S(2)}) collective-permute-start(bf16[192,384]{1,0:T(8,128)(2,1)} %get-tuple-element.78), channel_id=1, source_target_pairs={{0,64},{64,0},{1,65},{65,1},{2,66},{66,2},{3,67},{67,3},{4,68},{68... | collective-permute-start | bytes 442376 | tf_op jit(solution)/shard_map/ppermute | solution.py:32
  205.8 28.8 %collective-permute-start.47 = (bf16[3,256,384]{2,1,0:T(8,128)(2,1)S(1)}, bf16[3,256,384]{2,1,0:T(8,128)(2,1)S(1)}, u32[]{:S(2)}, u32[]{:S(2)}) collective-permute-start(bf16[3,256,384]{2,1,0:T(8,128)(2,1)S(1)} %copy-done), channel_id=1, source_target_pairs={{0,48},{16,32},{32,16},{48,0},{1,49},{17,33},{33,17},{49,1},{2,50}... | collective-permute-start | bytes 1769480 | tf_op jit(solution)/shard_map/ppermute | solution.py:32
  206.0 30.6 %collective-permute-start.46 = (bf16[3,256,384]{2,1,0:T(8,128)(2,1)S(1)}, bf16[3,256,384]{2,1,0:T(8,128)(2,1)S(1)}, u32[]{:S(2)}, u32[]{:S(2)}) collective-permute-start(bf16[3,256,384]{2,1,0:T(8,128)(2,1)S(1)} %copy-done), channel_id=1, source_target_pairs={{0,32},{16,48},{32,0},{48,16},{1,33},{17,49},{33,1},{49,17},{2,34}... | collective-permute-start | bytes 1769480 | tf_op jit(solution)/shard_map/ppermute | solution.py:32
  206.9 32.4 %collective-permute-start.45 = (bf16[3,256,384]{2,1,0:T(8,128)(2,1)S(1)}, bf16[3,256,384]{2,1,0:T(8,128)(2,1)}, u32[]{:S(2)}, u32[]{:S(2)}) collective-permute-start(bf16[3,256,384]{2,1,0:T(8,128)(2,1)S(1)} %copy-done), channel_id=1, source_target_pairs={{0,16},{16,0},{32,48},{48,32},{1,17},{17,1},{33,49},{49,33},{2,18}... | collective-permute-start | bytes 1769480 | tf_op jit(solution)/shard_map/ppermute | solution.py:32
  209.2 38.9 %collective-permute-start.30 = (bf16[4,256,384]{2,1,0:T(8,128)(2,1)}, bf16[4,256,384]{2,1,0:T(8,128)(2,1)S(1)}, u32[]{:S(2)}, u32[]{:S(2)}) collective-permute-start(bf16[4,256,384]{2,1,0:T(8,128)(2,1)} %get-tuple-element.50), channel_id=1, source_target_pairs={{0,1},{1,0},{2,3},{3,2},{4,5},{5,4},{6,7},{7,6},{8,9},{9,8},{10,11... | collective-permute-start | bytes 2359304 | tf_op jit(solution)/shard_map/ppermute | solution.py:32
  217.7 35.6 %collective-permute-start.27 = (bf16[256,384]{1,0:T(8,128)(2,1)}, bf16[256,384]{1,0:T(8,128)(2,1)}, u32[]{:S(2)}, u32[]{:S(2)}) collective-permute-start(bf16[256,384]{1,0:T(8,128)(2,1)} %get-tuple-element.68), channel_id=1, source_target_pairs={{0,2},{2,0},{4,6},{6,4},{1,3},{3,1},{5,7},{7,5},{8,10},{10,8},{12,... | collective-permute-start | bytes 589832 | tf_op jit(solution)/shard_map/ppermute | solution.py:32
  234.6 20.1 %collective-permute-start.29 = (bf16[256,384]{1,0:T(8,128)(2,1)}, bf16[256,384]{1,0:T(8,128)(2,1)}, u32[]{:S(2)}, u32[]{:S(2)}) collective-permute-start(bf16[256,384]{1,0:T(8,128)(2,1)} %get-tuple-element.69), channel_id=1, source_target_pairs={{0,6},{2,4},{4,2},{6,0},{1,7},{3,5},{5,3},{7,1},{8,14},{10,12},{12... | collective-permute-start | bytes 589832 | tf_op jit(solution)/shard_map/ppermute | solution.py:32
  237.4 18.6 %collective-permute-start.28 = (bf16[256,384]{1,0:T(8,128)(2,1)S(1)}, bf16[256,384]{1,0:T(8,128)(2,1)}, u32[]{:S(2)}, u32[]{:S(2)}) collective-permute-start(bf16[256,384]{1,0:T(8,128)(2,1)S(1)} %get-tuple-element.70), channel_id=1, source_target_pairs={{0,4},{2,6},{4,0},{6,2},{1,5},{3,7},{5,1},{7,3},{8,12},{10,14},{12... | collective-permute-start | bytes 589832 | tf_op jit(solution)/shard_map/ppermute | solution.py:32
  249.8 15.2 %collective-permute-start.48 = (bf16[3,192,384]{2,1,0:T(8,128)(2,1)S(1)}, bf16[3,192,384]{2,1,0:T(8,128)(2,1)S(1)}, u32[]{:S(2)}, u32[]{:S(2)}) collective-permute-start(bf16[3,192,384]{2,1,0:T(8,128)(2,1)S(1)} %get-tuple-element.62), channel_id=1, source_target_pairs={{0,8},{8,0},{1,9},{9,1},{2,10},{10,2},{3,11},{11,3},{4,12},{12,4},... | collective-permute-start | bytes 1327112 | tf_op jit(solution)/shard_map/ppermute | solution.py:32
  254.7 15.9 %collective-permute-start.49 = (bf16[3,192,384]{2,1,0:T(8,128)(2,1)S(1)}, bf16[3,192,384]{2,1,0:T(8,128)(2,1)S(1)}, u32[]{:S(2)}, u32[]{:S(2)}) collective-permute-start(bf16[3,192,384]{2,1,0:T(8,128)(2,1)S(1)} %get-tuple-element.64), channel_id=1, source_target_pairs={{0,64},{8,72},{1,65},{9,73},{2,66},{10,74},{3,67},{11,75},{4,68},{... | collective-permute-start | bytes 1327112 | tf_op jit(solution)/shard_map/ppermute | solution.py:32
  (72 other events, 483.3 us)
